TPU v7x, 256 devices: a whole 4x4x8 slice. The times are simulated.
256 devices in a mesh: rep: 8 (over x, z_lo), mp: 32 (over z_hi, y, core).
Axes of the slice: x: 4, y: 4, z: 8 (z_hi: 4, z_lo: 2; z = z_hi * 2 + z_lo), core: 2. Of those that a mesh axis runs over, the one named last changes fastest.
Arguments:
- tokens: bfloat16 [8, 2048, 5120], P('rep', 'mp'), may hold values from -6 to 6
- prompt_ids: int32 [8, 2048], P('rep', 'mp'), may hold values from 0 to 11, never falling along the last dimension, each value on 1 to 512 neighbouring positions
- modulation: float32 [8, 12, 3, 5120], P('rep'), may hold values from -4 to 4
- trainer_up: float32 [5120, 13824], P('mp', 'rep'), may hold values from -0.078125 to 0.078125
- trainer_down: float32 [13824, 5120], P('rep', 'mp'), may hold values from -0.0546875 to 0.0546875
Outputs:
- result: bfloat16 [8, 2048, 5120], P('rep', 'mp')
Inputs may be any that keep to these rules, and one draw needn't show every extreme that they name: `prompt_ids`: along each replica's 2048 tokens the prompt number never falls; each of the 12 prompts has at least one token, and one prompt has exactly a quarter of 2048.
All inputs are finite; a program needn't handle non-finite values.
Results may differ from a plain program's by a relative error of at most 0.023.
Values may be sent and summed in bfloat16 or wider, within the bound.
A program may use at most 192 MiB of HBM per device.

v0:
```python
import jax
import jax.numpy as jnp
import numpy as np
from jax import lax
from jax.sharding import Mesh, PartitionSpec as P

MP = ("mc", "core")


def local(tokens, prompt_ids, modulation, trainer_up, trainer_down):
    as_float = tokens[0].astype(jnp.float32)
    average = jnp.mean(as_float, axis=-1, keepdims=True)
    centred = as_float - average
    variance = jnp.mean(centred * centred, axis=-1, keepdims=True)
    normed = centred / jnp.sqrt(variance + 1e-06)
    prompts_here = modulation.shape[1]
    onehot = (prompt_ids[0][:, None] == jnp.arange(prompts_here, dtype=jnp.int32)[None, :]).astype(
        jnp.float32
    )
    chosen = jnp.einsum("tp,pkd->tkd", onehot, modulation[0], precision=lax.Precision.HIGHEST)
    shift = chosen[:, 0]
    scale = chosen[:, 1]
    gate = chosen[:, 2]
    xin = (normed * (1.0 + scale) + shift).astype(jnp.bfloat16)
    n_mp = lax.psum(1, MP)
    rows, cols = trainer_up.shape
    piece = cols // n_mp
    up_half = trainer_up.astype(jnp.bfloat16).reshape(rows, n_mp, piece).transpose(1, 0, 2)
    up_cols = lax.all_to_all(up_half, MP, 0, 0, tiled=True).reshape(n_mp * rows, piece)
    up_mine = lax.all_gather(up_cols, "rep", axis=1, tiled=True)
    up_other = lax.ppermute(up_mine, "core", [(0, 1), (1, 0)])
    w_up = jnp.concatenate([up_mine, up_other], axis=1)
    frows, dcols = trainer_down.shape
    down_half = trainer_down.astype(jnp.bfloat16).reshape(n_mp, piece, dcols)
    down_rows = lax.all_to_all(down_half, MP, 0, 0, tiled=True)
    down_rows = (
        down_rows.reshape(n_mp, piece, dcols).transpose(1, 0, 2).reshape(piece, n_mp * dcols)
    )
    down_mine = lax.all_gather(down_rows, "rep", axis=0, tiled=True)
    down_other = lax.ppermute(down_mine, "core", [(0, 1), (1, 0)])
    w_down = jnp.concatenate([down_mine, down_other], axis=0)
    x_all = lax.all_gather(xin, "mc", axis=0, tiled=True)
    hidden = jax.nn.gelu(
        jnp.dot(x_all, w_up, preferred_element_type=jnp.float32), approximate=True
    ).astype(jnp.bfloat16)
    mlp = lax.psum_scatter(
        jnp.dot(hidden, w_down, preferred_element_type=jnp.float32).astype(jnp.bfloat16),
        "mc",
        scatter_dimension=0,
        tiled=True,
    ).astype(jnp.float32)
    result = as_float + gate * mlp
    return result.astype(jnp.bfloat16)[None]


def solution(mesh):
    n_rep, n_mp = mesh.devices.shape
    chips = Mesh(mesh.devices.reshape(n_rep, n_mp // 2, 2), ("rep", "mc", "core"))
    in_specs = (
        P("rep", MP, None),
        P("rep", MP),
        P("rep", None, None, None),
        P(MP, "rep"),
        P("rep", MP),
    )
    out_specs = P("rep", MP, None)
    return jax.shard_map(local, mesh=chips, in_specs=in_specs, out_specs=out_specs, check_vma=False)
```

profile of v0, /device:TPU:1, one launch (start us, length us, event | category | flops | bytes accessed | tf_op | source)
XLA Modules:
  0.0 585.3 jit_solution(13966599562315707756)
XLA Ops:
  6.5 1.3 convert_element_type.31
  7.9 0.3 copy.13
  8.2 0.3 reshape.28
  8.5 37.6 %all_to_all.10 = bf16[32,160,54]{1,2,0:T(8,128)(2,1)S(1)} all-to-all(bf16[32,160,54]{1,2,0:T(8,128)(2,1)S(1)} %bitcast.65), channel_id=1, replica_groups=mesh['rep'=8,'mc'=16,'core'=2] {'mc','core'}, dimensions={0} | all-to-all | bytes 1105920 | tf_op jit(solution)/shard_map/all_to_all | solution.py:29
  46.3 2.3 reshape.29
  48.8 0.3 copy.15
  49.1 0.3 reshape.30
  49.4 41.0 %all_to_all.11 = bf16[32,54,160]{2,1,0:T(8,128)(2,1)S(1)} all-to-all(bf16[32,54,160]{2,1,0:T(8,128)(2,1)S(1)} %reshape.30), channel_id=1, replica_groups=mesh['rep'=8,'mc'=16,'core'=2] {'mc','core'}, dimensions={0} | all-to-all | bytes 1105920 | tf_op jit(solution)/shard_map/all_to_all | solution.py:35
  90.6 2.3 reshape.34
  93.2 0.3 fusion.21
  93.5 1.8 fusion.28
  95.3 1.9 copy-done
  97.3 1.2 fusion.27
  98.5 65.6 %all-gather.8.cloned.1.call-done = bf16[8,54,5120]{2,1,0:T(8,128)(2,1)} async-done(((bf16[1,54,5120]{2,1,0:T(8,128)(2,1)}), bf16[8,54,5120]{2,1,0:T(8,128)(2,1)}) %all-gather.8.cloned.1.call-update) | async-done | bytes 4423696 | tf_op jit(solution)/shard_map/all_gather | solution.py:30
  164.2 4.3 reshape.33
  168.5 0.5 collective-permute-start
  169.0 97.5 %all-gather.10.cloned.1.call-done = bf16[8,54,5120]{2,1,0:T(8,128)(2,1)} async-done(((bf16[1,54,5120]{2,1,0:T(8,128)(2,1)}), bf16[8,54,5120]{2,1,0:T(8,128)(2,1)}) %all-gather.10.cloned.1.call-update) | async-done | bytes 4423696 | tf_op jit(solution)/shard_map/all_gather | solution.py:39
  266.5 4.4 reshape.35
  270.9 0.9 collective-permute-start.1
  271.8 131.1 %all-gather.6.cloned.1.call-done = bf16[1024,5120]{1,0:T(8,128)(2,1)} async-done(((bf16[64,5120]{1,0:T(8,128)(2,1)}), bf16[1024,5120]{1,0:T(8,128)(2,1)}) %all-gather.6.cloned.1.call-update) | async-done | bytes 10485776 | tf_op jit(solution)/shard_map/all_gather | solution.py:42
  402.9 15.4 %fusion.14 = bf16[1024,864]{0,1:T(8,128)(2,1)S(1)} fusion(bf16[1024,5120]{1,0:T(8,128)(2,1)} %all-gather.6.cloned.1.call-done, bf16[5120,432]{0,1:T(8,128)(2,1)} %collective-permute-done, bf16[5120,432]{0,1:T(8,128)(2,1)} %bitcast.64), kind=kOutput, calls=%fused_computation.16 | convolution fusion | flops 9085353984 | bytes 21102592 | tf_op jit(solution)/shard_map/dot_general | solution.py:44
  418.4 16.2 %convolution_convert_fusion = bf16[1024,5120]{1,0:T(8,128)(2,1)} fusion(bf16[1024,864]{0,1:T(8,128)(2,1)S(1)} %fusion.14, bf16[432,5120]{1,0:T(8,128)(2,1)} %collective-permute-done.1, bf16[432,5120]{1,0:T(8,128)(2,1)S(1)} %copy-done.2), kind=kOutput, calls=%fused_computation | convolution fusion | flops 9082634240 | bytes 21102592 | tf_op jit(solution)/shard_map/dot_general | solution.py:47
  434.6 141.7 %reduce-scatter.2.cloned.1.call-done = bf16[64,5120]{1,0:T(8,128)(2,1)} async-done(((bf16[1024,5120]{1,0:T(8,128)(2,1)}), bf16[64,5120]{1,0:T(8,128)(2,1)}) %reduce-scatter.2.cloned.1.call-update) | async-done | bytes 655376 | tf_op jit(solution)/shard_map/reduce_scatter | solution.py:46
  576.2 2.6 fusion.31
  (27 shorter events, 0.9 us)
Async XLA Ops:
  6.5 157.6 %all-gather.8.cloned.1.call-start = ((), (), s32[]{:S(2)}) async-start(), calls=%async_computation.5 | async-start | bytes 5160960 | tf_op jit(solution)/shard_map/all_gather | solution.py:30
  8.4 40.3 %copy-start.4 = (f32[1728,160]{0,1:T(8,128)S(1)}, f32[1728,160]{0,1:T(8,128)}, u32[]{:S(2)}) copy-start(f32[1728,160]{0,1:T(8,128)} %param.9) | copy-start | bytes 3317764
  48.7 217.8 %all-gather.10.cloned.1.call-start = ((), (), s32[]{:S(2)}) async-start(), calls=%async_computation.6 | async-start | bytes 5160960 | tf_op jit(solution)/shard_map/all_gather | solution.py:39
  49.1 43.8 %copy-start.1 = (bf16[1,64,5120]{2,1,0:T(8,128)(2,1)S(1)}, bf16[1,64,5120]{2,1,0:T(8,128)(2,1)}, u32[]{:S(2)}) copy-start(bf16[1,64,5120]{2,1,0:T(8,128)(2,1)} %param.5) | copy-start | bytes 1966084
  49.4 44.1 %copy-start.3 = (f32[1,12,3,5120]{3,0,2,1:T(1,128)S(1)}, f32[1,12,3,5120]{3,0,2,1:T(1,128)}, u32[]{:S(2)}) copy-start(f32[1,12,3,5120]{3,0,2,1:T(1,128)} %param.7) | copy-start | bytes 2211844
  49.4 44.1 %copy-start.5 = (s32[1,64]{1,0:T(1,128)S(1)}, s32[1,64]{1,0:T(1,128)}, u32[]{:S(2)}) copy-start(s32[1,64]{1,0:T(1,128)} %param.6) | copy-start | bytes 772
  92.9 310.0 %all-gather.6.cloned.1.call-start = ((), (), s32[]{:S(2)}) async-start(), calls=%async_computation.3 | async-start | bytes 11141120 | tf_op jit(solution)/shard_map/all_gather | solution.py:42
  95.3 1.9 copy-start
  98.5 477.7 %reduce-scatter.2.cloned.1.call-start = ((), (), s32[]{:S(2)}) async-start(), calls=%async_computation.4 | async-start | bytes 11141120 | tf_op jit(solution)/shard_map/reduce_scatter | solution.py:46
  168.5 103.3 %collective-permute-start = (bf16[5120,432]{0,1:T(8,128)(2,1)}, bf16[5120,432]{0,1:T(8,128)(2,1)}, u32[]{:S(2)}, u32[]{:S(2)}) collective-permute-start(bf16[5120,432]{0,1:T(8,128)(2,1)} %bitcast.63), channel_id=1, source_target_pairs={{0,1},{1,0},{2,3},{3,2},{4,5},{5,4},{6,7},{7,6},{8,9},{9,8},{10,11... | collective-permute-start | bytes 13271048 | tf_op jit(solution)/shard_map/ppermute | solution.py:31
  270.9 147.5 %collective-permute-start.1 = (bf16[432,5120]{1,0:T(8,128)(2,1)}, bf16[432,5120]{1,0:T(8,128)(2,1)}, u32[]{:S(2)}, u32[]{:S(2)}) collective-permute-start(bf16[432,5120]{1,0:T(8,128)(2,1)} %reshape.35), channel_id=1, source_target_pairs={{0,1},{1,0},{2,3},{3,2},{4,5},{5,4},{6,7},{7,6},{8,9},{9,8},{10,11... | collective-permute-start | bytes 13271048 | tf_op jit(solution)/shard_map/ppermute | solution.py:40
  402.9 15.5 %copy-start.2 = (bf16[432,5120]{1,0:T(8,128)(2,1)S(1)}, bf16[432,5120]{1,0:T(8,128)(2,1)}, u32[]{:S(2)}) copy-start(bf16[432,5120]{1,0:T(8,128)(2,1)} %reshape.35) | copy-start | bytes 13271044
Sparse Core Ops, SparseCore 0:
  48.8 115.3 all-gather.7
  166.0 100.4 all-gather.9
  268.9 133.9 all-gather.5
  434.7 141.4 reduce-scatter.1
where the time goes:
time: 586 us; the launch traced here: 585 us
  waiting for transfers between devices  436 us (74%)
  blocking collectives  78.6 us (13%)
  matrix products  33.4 us (6%)
  local copies, waits for them, and re-layouts  16.9 us (3%)
  between operations  13.3 us (2%)
    reduce_scatter x1, waiting for transfers between devices, local(): lax.psum_scatter(jnp.dot(hidden, w_down, preferred_element_type=jnp.float...  142 us
    all_gather x1, waiting for transfers between devices, local(): x_all = lax.all_gather(xin, 'mc', axis=0, tiled=True)  131 us
    all_gather x1, waiting for transfers between devices, local(): down_mine = lax.all_gather(down_rows, 'rep', axis=0, tiled=True)  97.5 us
    all_gather x1, waiting for transfers between devices, local(): up_mine = lax.all_gather(up_cols, 'rep', axis=1, tiled=True)  65.6 us
    all_to_all x1, blocking collectives, local(): down_rows = lax.all_to_all(down_half, MP, 0, 0, tiled=True)  41 us
    all_to_all x1, blocking collectives, local(): lax.all_to_all(up_half, MP, 0, 0, tiled=True).reshape(n_mp * rows, piece)  37.6 us
    dot_general x1, matrix products, local(): jnp.dot(hidden, w_down, preferred_element_type=jnp.float32)  16.2 us
    dot_general x1, matrix products, local(): jnp.dot(x_all, w_up, preferred_element_type=jnp.float32)  15.4 us
  transfers between devices with their start and end apart: 6, of which 4 were waited for; matrix products, arithmetic and copies ran while one was open for 5% of the time, Pallas kernels for 0%

commit v1 on v0

--- a/solution.py
+++ b/solution.py
@@ -39,7 +39,9 @@
     down_mine = lax.all_gather(down_rows, "rep", axis=0, tiled=True)
     down_other = lax.ppermute(down_mine, "core", [(0, 1), (1, 0)])
     w_down = jnp.concatenate([down_mine, down_other], axis=0)
-    x_all = lax.all_gather(xin, "mc", axis=0, tiled=True)
+    x_all = jnp.concatenate(
+        lax.all_to_all(jnp.stack(lax.psum(1, "mc") * [xin]), "mc", 0, 0), axis=0
+    )
     hidden = jax.nn.gelu(
         jnp.dot(x_all, w_up, preferred_element_type=jnp.float32), approximate=True
     ).astype(jnp.bfloat16)

time: 586 us -> 674 us (1.15)
  waiting for transfers between devices: 436 us -> 571 us
  blocking collectives: 78.6 us -> 0 us
  starting transfers between devices: 1.52 us -> 25.2 us
    all_gather x1, waiting for transfers between devices: 65.6 us -> 288 us  [local(): up_mine = lax.all_gather(up_cols, 'rep', axis=1, tiled=True)]
    all_gather x1 -> x0, waiting for transfers between devices: 131 us -> none  [local(): x_all = lax.all_gather(xin, 'mc', axis=0, tiled=True)]
    all_to_all x2 -> x0, blocking collectives: 78.6 us -> none  [the longest x1 41 us: local(): down_rows = lax.all_to_all(down_half, MP, 0, 0, tiled=True)]
    all_to_all x0 -> x3, waiting for transfers between devices: none -> 41.6 us  [the longest x1 23.8 us: local(): down_rows = lax.all_to_all(down_half, MP, 0, 0, tiled=True)]
    all_to_all x0 -> x3, starting transfers between devices: none -> 24.1 us  [the longest x1 12.9 us: local(): lax.all_to_all(up_half, MP, 0, 0, tiled=True).reshape(n_mp * rows, piece)]
  transfers between devices with their start and end apart: 6 -> 8, of which waited for: 4 -> 5; matrix products, arithmetic and copies ran while one was open for 5% -> 6% of each run, Pallas kernels for 0% -> 0%
where the time goes in v1:
time: 674 us
  waiting for transfers between devices  571 us (85%)
  matrix products  35.2 us (5%)
  starting transfers between devices  25.2 us (4%)
  local copies, waits for them, and re-layouts  21.9 us (3%)
  between operations  13.2 us (2%)
  other arithmetic  7.83 us (1%)
    all_gather x1, waiting for transfers between devices, local(): up_mine = lax.all_gather(up_cols, 'rep', axis=1, tiled=True)  288 us
    reduce_scatter x1, waiting for transfers between devices, local(): lax.psum_scatter(jnp.dot(hidden, w_down, preferred_element_type=jnp.float...  138 us
    all_gather x1, waiting for transfers between devices, local(): down_mine = lax.all_gather(down_rows, 'rep', axis=0, tiled=True)  103 us
    all_to_all x1, waiting for transfers between devices, local(): down_rows = lax.all_to_all(down_half, MP, 0, 0, tiled=True)  23.8 us
    all_to_all x1, waiting for transfers between devices, local(): lax.all_to_all(up_half, MP, 0, 0, tiled=True).reshape(n_mp * rows, piece)  17.8 us
    dot_general x1, matrix products, local(): jnp.dot(hidden, w_down, preferred_element_type=jnp.float32)  16.2 us
    dot_general x1, matrix products, local(): jnp.dot(x_all, w_up, preferred_element_type=jnp.float32)  15.4 us
  transfers between devices with their start and end apart: 8, of which 5 were waited for; matrix products, arithmetic and copies ran while one was open for 6% of the time, Pallas kernels for 0%

profile of v1, /device:TPU:1, one launch (start us, length us, event | category | flops | bytes accessed | tf_op | source)
XLA Modules:
  0.0 673.9 jit_solution(15452978305372123046)
XLA Ops:
  6.5 1.3 convert_element_type.33
  8.2 1.2 reshape.58
  9.4 12.9 %all-to-all-start.1 = ((bf16[32,160,54]{1,2,0:T(8,128)(2,1)}), bf16[32,160,54]{1,2,0:T(8,128)(2,1)S(1)}, u32[]{:S(2)}, u32[]{:S(2)}) async-start(bf16[32,160,54]{1,2,0:T(8,128)(2,1)} %bitcast.9), calls=%async_computation.1 | async-start | bytes 1835008 | tf_op jit(solution)/shard_map/all_to_all | solution.py:29
  22.3 1.3 convert_element_type.35
  23.9 1.2 reshape.60
  25.8 3.6 fusion.28
  29.4 17.8 %all-to-all-done.1 = bf16[32,160,54]{1,2,0:T(8,128)(2,1)S(1)} async-done(((bf16[32,160,54]{1,2,0:T(8,128)(2,1)}), bf16[32,160,54]{1,2,0:T(8,128)(2,1)S(1)}, u32[]{:S(2)}, u32[]{:S(2)}) %all-to-all-start.1) | async-done | bytes 552992 | tf_op jit(solution)/shard_map/all_to_all | solution.py:29
  47.2 6.4 all-to-all-start.2
  53.6 2.1 fusion.32
  55.7 23.8 %all-to-all-done.2 = bf16[32,54,160]{2,1,0:T(8,128)(2,1)S(1)} async-done(((bf16[32,54,160]{2,1,0:T(8,128)(2,1)}), bf16[32,54,160]{2,1,0:T(8,128)(2,1)S(1)}, u32[]{:S(2)}, u32[]{:S(2)}) %all-to-all-start.2) | async-done | bytes 552992 | tf_op jit(solution)/shard_map/all_to_all | solution.py:35
  79.5 5.1 stack.5
  84.6 4.8 all-to-all-start
  89.7 2.3 reshape.59
  92.3 2.3 reshape.64
  94.7 288.2 %all-gather.5.cloned.1.call-done = bf16[8,54,5120]{2,1,0:T(8,128)(2,1)} async-done(((bf16[1,54,5120]{2,1,0:T(8,128)(2,1)}), bf16[8,54,5120]{2,1,0:T(8,128)(2,1)}) %all-gather.5.cloned.1.call-update) | async-done | bytes 4423696 | tf_op jit(solution)/shard_map/all_gather | solution.py:30
  382.8 4.3 reshape.63
  387.1 0.5 collective-permute-start
  387.6 102.6 %all-gather.7.cloned.1.call-done = bf16[8,54,5120]{2,1,0:T(8,128)(2,1)} async-done(((bf16[1,54,5120]{2,1,0:T(8,128)(2,1)}), bf16[8,54,5120]{2,1,0:T(8,128)(2,1)}) %all-gather.7.cloned.1.call-update) | async-done | bytes 4423696 | tf_op jit(solution)/shard_map/all_gather | solution.py:39
  490.2 4.4 reshape.65
  494.6 0.4 collective-permute-start.1
  495.1 15.4 %fusion.14 = bf16[1024,864]{0,1:T(8,128)(2,1)S(1)} fusion(bf16[1024,5120]{1,0:T(8,128)(2,1)} %bitcast.8, bf16[5120,432]{0,1:T(8,128)(2,1)} %collective-permute-done, bf16[5120,432]{0,1:T(8,128)(2,1)} %bitcast.63), kind=kOutput, calls=%fused_computation.16 | convolution fusion | flops 9085353984 | bytes 21102592 | tf_op jit(solution)/shard_map/dot_general | solution.py:46
  510.5 16.2 %convolution_convert_fusion = bf16[1024,5120]{1,0:T(8,128)(2,1)} fusion(bf16[1024,864]{0,1:T(8,128)(2,1)S(1)} %fusion.14, bf16[432,5120]{1,0:T(8,128)(2,1)} %collective-permute-done.1, bf16[432,5120]{1,0:T(8,128)(2,1)S(1)} %copy-done.1), kind=kOutput, calls=%fused_computation | convolution fusion | flops 9082634240 | bytes 21102592 | tf_op jit(solution)/shard_map/dot_general | solution.py:49
  526.7 138.1 %reduce-scatter.2.cloned.1.call-done = bf16[64,5120]{1,0:T(8,128)(2,1)} async-done(((bf16[1024,5120]{1,0:T(8,128)(2,1)}), bf16[64,5120]{1,0:T(8,128)(2,1)}) %reduce-scatter.2.cloned.1.call-update) | async-done | bytes 655376 | tf_op jit(solution)/shard_map/reduce_scatter | solution.py:48
  664.9 2.6 fusion.31
  (25 shorter events, 1.8 us)
Async XLA Ops:
  9.4 15.8 %copy-start = (bf16[1,64,5120]{2,1,0:T(8,128)(2,1)S(1)}, bf16[1,64,5120]{2,1,0:T(8,128)(2,1)}, u32[]{:S(2)}) copy-start(bf16[1,64,5120]{2,1,0:T(8,128)(2,1)} %param.5) | copy-start | bytes 1966084
  9.4 37.8 %all-to-all-start.1 = ((bf16[32,160,54]{1,2,0:T(8,128)(2,1)}), bf16[32,160,54]{1,2,0:T(8,128)(2,1)S(1)}, u32[]{:S(2)}, u32[]{:S(2)}) async-start(bf16[32,160,54]{1,2,0:T(8,128)(2,1)} %bitcast.9), calls=%async_computation.1 | async-start | bytes 1835008 | tf_op jit(solution)/shard_map/all_to_all | solution.py:29
  22.3 3.5 copy-start.3
  23.9 1.8 copy-start.2
  47.2 32.3 %all-to-all-start.2 = ((bf16[32,54,160]{2,1,0:T(8,128)(2,1)}), bf16[32,54,160]{2,1,0:T(8,128)(2,1)S(1)}, u32[]{:S(2)}, u32[]{:S(2)}) async-start(bf16[32,54,160]{2,1,0:T(8,128)(2,1)} %reshape.60), calls=%async_computation.2 | async-start | bytes 1835008 | tf_op jit(solution)/shard_map/all_to_all | solution.py:35
  84.6 410.4 %all-to-all-start = ((bf16[16,64,5120]{2,1,0:T(8,128)(2,1)}), bf16[16,64,5120]{2,1,0:T(8,128)(2,1)}, u32[]{:S(2)}, u32[]{:S(2)}) async-start(bf16[16,64,5120]{2,1,0:T(8,128)(2,1)} %stack.5), calls=%async_computation | async-start | bytes 20971520 | tf_op jit(solution)/shard_map/all_to_all | solution.py:43
  89.4 293.4 %all-gather.5.cloned.1.call-start = ((), (), s32[]{:S(2)}) async-start(), calls=%async_computation.5 | async-start | bytes 5160960 | tf_op jit(solution)/shard_map/all_gather | solution.py:30
  92.0 398.2 %all-gather.7.cloned.1.call-start = ((), (), s32[]{:S(2)}) async-start(), calls=%async_computation.6 | async-start | bytes 5160960 | tf_op jit(solution)/shard_map/all_gather | solution.py:39
  94.6 570.2 %reduce-scatter.2.cloned.1.call-start = ((), (), s32[]{:S(2)}) async-start(), calls=%async_computation.4 | async-start | bytes 11141120 | tf_op jit(solution)/shard_map/reduce_scatter | solution.py:48
  387.1 107.9 %collective-permute-start = (bf16[5120,432]{0,1:T(8,128)(2,1)}, bf16[5120,432]{0,1:T(8,128)(2,1)}, u32[]{:S(2)}, u32[]{:S(2)}) collective-permute-start(bf16[5120,432]{0,1:T(8,128)(2,1)} %bitcast.62), channel_id=1, source_target_pairs={{0,1},{1,0},{2,3},{3,2},{4,5},{5,4},{6,7},{7,6},{8,9},{9,8},{10,11... | collective-permute-start | bytes 13271048 | tf_op jit(solution)/shard_map/ppermute | solution.py:31
  494.6 15.9 %collective-permute-start.1 = (bf16[432,5120]{1,0:T(8,128)(2,1)}, bf16[432,5120]{1,0:T(8,128)(2,1)}, u32[]{:S(2)}, u32[]{:S(2)}) collective-permute-start(bf16[432,5120]{1,0:T(8,128)(2,1)} %reshape.65), channel_id=1, source_target_pairs={{0,1},{1,0},{2,3},{3,2},{4,5},{5,4},{6,7},{7,6},{8,9},{9,8},{10,11... | collective-permute-start | bytes 13271048 | tf_op jit(solution)/shard_map/ppermute | solution.py:40
  495.0 15.5 %copy-start.1 = (bf16[432,5120]{1,0:T(8,128)(2,1)S(1)}, bf16[432,5120]{1,0:T(8,128)(2,1)}, u32[]{:S(2)}) copy-start(bf16[432,5120]{1,0:T(8,128)(2,1)} %reshape.65) | copy-start | bytes 13271044
Sparse Core Ops, SparseCore 0:
  92.1 290.6 all-gather.4
  384.6 105.5 all-gather.6
  526.8 137.9 reduce-scatter.1
